TPU v7x, 32 devices: a whole 2x2x4 slice. The times are simulated.
32 devices in a mesh: row: 2 (over y), col: 4 (over z), layer: 4 (over x, core).
Axes of the slice: x: 2, y: 2, z: 4, core: 2. Of those that a mesh axis runs over, the one named last changes fastest.
Arguments:
- integrals: bfloat16 [64, 1024, 768], P('layer', 'col', 'row'), may hold values from -0.0234375 to 0.0234375
- amplitudes: bfloat16 [64, 1024, 512], P('layer', 'row', 'col'), may hold values from -6 to 6
- coulomb: bfloat16 [768, 512], P(('row', 'layer'), 'col'), may hold values from -6 to 6
- row_gap: float32 [768], P(('row', 'layer')), may hold values from 0.5 to 4
- col_gap: float32 [512], P('col'), may hold values from 0.5 to 4
Outputs:
- residual: float32 [768, 512], P(('row', 'layer'), 'col')
All inputs are finite; a program needn't handle non-finite values.
Results may differ from a plain program's by a relative error of at most 0.0003.
Values may be sent and summed in bfloat16 or wider, within the bound.
A program may use at most 64 MiB of HBM per device.

v0:
```python
import jax
import jax.numpy as jnp
from jax import lax
from jax.sharding import PartitionSpec as P


def local(integrals, amplitudes, coulomb, row_gap, col_gap):
    contract = (((0, 1), (0, 1)), ((), ()))
    gathered = lax.all_gather(amplitudes, "row", axis=1, tiled=True)
    partial_sum = lax.dot_general(
        lax.all_gather(integrals, "col", axis=1, tiled=True),
        gathered,
        contract,
        preferred_element_type=jnp.float32,
    )
    own_rows = lax.psum_scatter(partial_sum, "layer", scatter_dimension=0, tiled=True)
    gap_sum = row_gap[:, None] + col_gap[None, :]
    return (coulomb.astype(jnp.float32) + own_rows) / gap_sum


def solution(mesh):
    placed = (
        P("layer", "col", "row"),
        P("layer", "row", "col"),
        P(("row", "layer"), "col"),
        P(("row", "layer")),
        P("col"),
    )
    return jax.shard_map(
        local, mesh=mesh, in_specs=placed, out_specs=P(("row", "layer"), "col"), check_vma=False
    )
```

profile of v0, /device:TPU:0, one launch (start us, length us, event | category | flops | bytes accessed | tf_op | source)
XLA Modules:
  0.0 323.7 jit_solution(6557255754955836861)
XLA Ops:
  6.5 0.0 all-gather.5.cloned.1.call-start
  6.5 0.7 all-gather.5.cloned.1.call-update
  7.3 0.0 all-gather.3.cloned.1.call-start
  7.3 4.6 %copy.6 = bf16[16,256,384]{1,2,0:T(8,128)(2,1)} copy(bf16[16,256,384]{2,1,0:T(8,128)(2,1)} %param.5) | data formatting | bytes 6291456 | tf_op args[0]
  11.9 0.0 all-gather.3.cloned.1.call-update
  12.0 0.0 copy-start
  12.0 0.0 copy-start.1
  12.0 0.0 copy-start.2
  12.0 0.0 reduce-scatter.2.cloned.1.call-start
  12.1 56.3 %all-gather.5.cloned.1.call-done = bf16[16,1024,128]{2,1,0:T(8,128)(2,1)} async-done(((bf16[16,512,128]{2,1,0:T(8,128)(2,1)}), bf16[16,1024,128]{2,1,0:T(8,128)(2,1)}) %all-gather.5.cloned.1.call-update) | async-done | bytes 4194320 | tf_op jit(solution)/shard_map/all_gather | solution.py:9
  68.4 219.3 %all-gather.3.cloned.1.call-done = bf16[16,1024,384]{1,2,0:T(8,128)(2,1)} async-done(((bf16[16,256,384]{1,2,0:T(8,128)(2,1)}), bf16[16,1024,384]{1,2,0:T(8,128)(2,1)}) %all-gather.3.cloned.1.call-update) | async-done | bytes 12582928 | tf_op jit(solution)/shard_map/all_gather | solution.py:11
  287.6 9.9 %convolution_bitcast_fusion = f32[384,128]{1,0:T(8,128)} fusion(bf16[16,1024,384]{1,2,0:T(8,128)(2,1)} %all-gather.3.cloned.1.call-done, bf16[16,1024,128]{2,1,0:T(8,128)(2,1)} %all-gather.5.cloned.1.call-done), kind=kOutput, calls=%fused_computation | convolution fusion | flops 1610612736 | bytes 16973824 | tf_op jit(solution)/shard_map/dot_general | solution.py:10
  297.5 0.0 reduce-scatter.2.cloned.1.call-update
  297.5 18.1 %reduce-scatter.2.cloned.1.call-done = f32[96,128]{1,0:T(8,128)} async-done(((f32[384,128]{1,0:T(8,128)}), f32[96,128]{1,0:T(8,128)}) %reduce-scatter.2.cloned.1.call-update) | async-done | bytes 49168 | tf_op jit(solution)/shard_map/reduce_scatter | solution.py:16
  315.6 0.0 copy-done
  315.6 0.0 copy-done.1
  315.6 0.0 copy-done.2
  315.6 1.5 add_divide_fusion
Async XLA Ops:
  6.5 61.8 %all-gather.5.cloned.1.call-start = ((), (), s32[]{:S(2)}) async-start(), calls=%async_computation.2 | async-start | bytes 6291456 | tf_op jit(solution)/shard_map/all_gather | solution.py:9
  7.3 280.4 %all-gather.3.cloned.1.call-start = ((), (), s32[]{:S(2)}) async-start(), calls=%async_computation.1 | async-start | bytes 15728640 | tf_op jit(solution)/shard_map/all_gather | solution.py:11
  12.0 303.6 %copy-start = (bf16[96,128]{1,0:T(8,128)(2,1)S(1)}, bf16[96,128]{1,0:T(8,128)(2,1)}, u32[]{:S(2)}) copy-start(bf16[96,128]{1,0:T(8,128)(2,1)} %param.7) | copy-start | bytes 73732
  12.0 303.6 %copy-start.1 = (f32[128]{0:T(128)S(1)}, f32[128]{0:T(128)}, u32[]{:S(2)}) copy-start(f32[128]{0:T(128)} %param.9) | copy-start | bytes 1540
  12.0 303.6 %copy-start.2 = (f32[96]{0:T(128)S(1)}, f32[96]{0:T(128)}, u32[]{:S(2)}) copy-start(f32[96]{0:T(128)} %param.8) | copy-start | bytes 1156
  12.0 303.6 %reduce-scatter.2.cloned.1.call-start = ((), (), s32[]{:S(2)}) async-start(), calls=%async_computation.3 | async-start | bytes 245760 | tf_op jit(solution)/shard_map/reduce_scatter | solution.py:16
Sparse Core Ops, SparseCore 0:
  8.9 59.4 all-gather.4
  69.9 217.6 all-gather.2
  297.6 17.9 reduce-scatter.1
where the time goes:
time: 324 us
  waiting for transfers between devices  294 us (91%)
  between operations  13.1 us (4%)
  matrix products  9.85 us (3%)
  local copies, waits for them, and re-layouts  4.66 us (1%)
    all_gather x1, waiting for transfers between devices, local(): lax.all_gather(integrals, 'col', axis=1, tiled=True)  219 us
    all_gather x1, waiting for transfers between devices, local(): gathered = lax.all_gather(amplitudes, 'row', axis=1, tiled=True)  56.3 us
    reduce_scatter x1, waiting for transfers between devices, local(): lax.psum_scatter(partial_sum, 'layer', scatter_dimension=0, tiled=True)  18.1 us
    dot_general x1, matrix products, local(): lax.dot_general(lax.all_gather(integrals, 'col', axis=1, tiled=True), gat...  9.85 us
  transfers between devices with their start and end apart: 3, of which 3 were waited for; matrix products, arithmetic and copies ran while one was open for 1% of the time, Pallas kernels for 0%

commit v1 on v0

v1 whole, which is shorter than its diff:
```python
import functools

import jax
import jax.numpy as jnp
from jax import lax
from jax.experimental import pallas as pl
from jax.experimental.pallas import tpu as pltpu
from jax.sharding import PartitionSpec as P

CHUNKS = 8


def kernel(R, C, L, Q, i_ref, a_ref, coul_ref, rgap_ref, cgap_ref, o_ref,
           a_all, az, relay, i_buf, i_t, acc, lay_buf, col_buf,
           ysend, yrecv, zsend, zrecv, hsend, hrecv, fsend, frecv, isem,
           lsend, lrecv, csend, crecv):
    r, c, l = lax.axis_index("row"), lax.axis_index("col"), lax.axis_index("layer")
    K, V_row, N = a_ref.shape
    V = i_ref.shape[1]
    M = i_ref.shape[2]
    kc = K // Q
    m = C // R
    half = V // 2
    rows = M // L
    stages = L.bit_length() - 1
    far = C // 2 if C % 2 == 0 and C >= 4 else 0

    def dev(row=None, col=None, layer=None):
        return {"row": r if row is None else row, "col": c if col is None else col, "layer": l if layer is None else layer}

    def remote(src, dst, ss, rs, to):
        return pltpu.make_async_remote_copy(src_ref=src, dst_ref=dst, send_sem=ss, recv_sem=rs,
                                            device_id=to, device_id_type=pl.DeviceIdType.MESH)

    def ks(q):
        return pl.ds(q * kc, kc)

    def near(dc):
        return lax.rem(c + dc + C, C)

    def i_copy(q):
        return pltpu.make_async_copy(i_ref.at[ks(q)], i_buf.at[ks(q)], isem.at[q])

    def own_copy(q):
        return pltpu.make_async_copy(a_ref.at[ks(q)], a_all.at[r, ks(q)], yrecv.at[r, q])

    for q in range(Q):
        own_copy(q).start()
        i_copy(q).start()

    barrier = pltpu.get_barrier_semaphore()
    partners = [dev(row=lax.rem(r + d, R)) for d in range(1, R)]
    partners += [dev(col=near(d)) for d in range(1, C)]
    partners += [dev(layer=l ^ (1 << t)) for t in range(stages)]
    for p in partners:
        pl.semaphore_signal(barrier, inc=1, device_id=p, device_id_type=pl.DeviceIdType.MESH)
    pl.semaphore_wait(barrier, len(partners))

    def y_copy(d, q):
        to = lax.rem(r + d, R)
        return remote(a_ref.at[ks(q)], a_all.at[r, ks(q)], ysend.at[d, q], yrecv.at[r, q], dev(row=to))

    def y_wait(d, q):
        s = lax.rem(r + d, R)
        remote(a_ref.at[ks(q)], a_all.at[s, ks(q)], ysend.at[0, q], yrecv.at[s, q], dev(row=s)).wait_recv()

    def z_copies(dc, q, src, offset):
        b = near(dc)
        if far and dc == far:
            out = []
            for side in range(2):
                part = src.at[ks(q), pl.ds(pl.multiple_of(offset + side * half, half), half)]
                out.append(remote(part, relay.at[side, ks(q)], hsend.at[side, q], hrecv.at[side, q],
                                  dev(col=near(1 - 2 * side))))
            return out
        part = src.at[ks(q), pl.ds(pl.multiple_of(offset, V), V)]
        return [remote(part, az.at[c, ks(q)], zsend.at[dc, q], zrecv.at[c, q], dev(col=b))]

    order = ([far] if far else []) + [d for k in range(1, C) for d in ((k, C - k) if k < C - k else (k,) if k == C - k else ()) if d != far]

    for q in range(Q):
        for d in range(1, R):
            y_copy(d, q).start()
        for dc in order:
            b = near(dc)

            @pl.when(lax.div(b, m) == r)
            def _():
                for cp in z_copies(dc, q, a_ref, lax.rem(b, m) * V):
                    cp.start()

    def late(q):
        for d in range(1, R):
            y_wait(d, q)
        for dc in order:
            b = near(dc)

            @pl.when(lax.div(b, m) != r)
            def _():
                for cp in z_copies(dc, q, a_all.at[lax.div(b, m)], lax.rem(b, m) * V):
                    cp.start()

    def forward_copy(side, q):
        s = near(-1 + 2 * side)
        to = near((far - 1) * (1 - 2 * side))
        return remote(relay.at[side, ks(q)], az.at[s, ks(q), pl.ds(side * half, half)],
                      fsend.at[side, q], frecv.at[side, q], dev(col=to))

    def forward(q):
        if not far:
            return
        for side in range(2):
            remote(relay.at[side, ks(q)], relay.at[side, ks(q)], hsend.at[side, q], hrecv.at[side, q],
                   dev(col=near(1))).wait_recv()
            forward_copy(side, q).start()

    def add(block, x, q):
        w = kc * V
        part = lax.dot_general(i_t[:, q * w:(q + 1) * w], x.reshape(w, N), (((1,), (0,)), ((), ())),
                               preferred_element_type=jnp.float32)
        for lb in range(L):
            piece = part[lb * rows:(lb + 1) * rows]
            if q == 0:
                acc[lb, block] = piece
            else:
                acc[lb, block] += piece

    def own_product(q):
        i_copy(q).wait()
        for k in range(kc):
            at = (q * kc + k) * V
            i_t[:, at:at + V] = i_buf[q * kc + k].T
        own_copy(q).wait()
        x = a_all[lax.div(c, m), ks(q), pl.ds(pl.multiple_of(lax.rem(c, m) * V, V), V)]
        add(c, x, q)

    def arrived(q):
        for dc in order[::-1]:
            s = near(-dc)
            if far and dc == far:
                for side in range(2):
                    dst = az.at[s, ks(q), pl.ds(side * half, half)]
                    remote(dst, dst, fsend.at[side, q], frecv.at[side, q], dev(col=near(1))).wait_recv()
            else:
                remote(az.at[s, ks(q)], az.at[s, ks(q)], zsend.at[dc, q], zrecv.at[s, q], dev(col=near(1))).wait_recv()
            add(s, az[s, ks(q)], q)

    for step in range(Q + 2):
        if step < Q:
            late(step)
        if 1 <= step <= Q:
            forward(step - 1)
        if step < Q:
            own_product(step)
        if step >= 2:
            arrived(step - 2)

    c_order = order + [0]

    def block(t, hi, bit):
        return (hi << (t + 1)) | (bit << t) | (l & ((1 << t) - 1))

    def hi_order(n):
        if n == 1:
            return [0]
        below = hi_order(n // 2)
        return [2 * x + 1 for x in below] + [2 * x for x in below]

    def halving(t, i, dc):
        n = L >> (t + 1)
        hi = (l >> (t + 1)) ^ hi_order(n)[i]
        bit = (l >> t) & 1
        col = near(dc)
        slot = n - 1 + hi
        sem = (slot, col)
        return (remote(acc.at[block(t, hi, 1 - bit), col], lay_buf.at[slot, col], lsend.at[sem], lrecv.at[sem],
                       dev(layer=l ^ (1 << t))), block(t, hi, bit), slot, col)

    def final_copy(dc):
        return remote(acc.at[l, near(dc)], col_buf.at[c], csend.at[dc], crecv.at[c], dev(col=near(dc)))

    for i in range(L >> 1):
        for dc in c_order:
            halving(0, i, dc)[0].start()
    for t in range(stages):
        for i in range(L >> (t + 1)):
            for dc in c_order:
                cp, keep, slot, col = halving(t, i, dc)
                cp.wait_recv()
                acc[keep, col] += lay_buf[slot, col]
                if t + 1 < stages:
                    n = L >> (t + 2)
                    if i < n:
                        halving(t + 1, i, dc)[0].start()
                elif dc:
                    final_copy(dc).start()

    total = acc[l, c]
    for dc in order[::-1]:
        s = near(-dc)
        remote(col_buf.at[s], col_buf.at[s], csend.at[dc], crecv.at[s], dev(col=near(1))).wait_recv()
        total += col_buf[s]
    o_ref[...] = (coul_ref[...].astype(jnp.float32) + total) / (rgap_ref[...] + cgap_ref[...])

    for q in range(Q):
        for d in range(1, R):
            y_copy(d, q).wait_send()
        for dc in order:
            for cp in z_copies(dc, q, a_ref, 0):
                cp.wait_send()
        if far:
            for side in range(2):
                forward_copy(side, q).wait_send()
    for t in range(stages):
        for i in range(L >> (t + 1)):
            for dc in c_order:
                halving(t, i, dc)[0].wait_send()
    for dc in order:
        final_copy(dc).wait_send()


def local(R, C, L, integrals, amplitudes, coulomb, row_gap, col_gap):
    K, V, M = integrals.shape
    V_row, N = amplitudes.shape[1:]
    rows = M // L
    Q = CHUNKS
    while K % Q:
        Q -= 1
    slots = L - 1
    dma = pltpu.SemaphoreType.DMA
    vmem = pl.BlockSpec(memory_space=pltpu.VMEM)
    anyspace = pl.BlockSpec(memory_space=pl.ANY)
    return pl.pallas_call(
        functools.partial(kernel, R, C, L, Q),
        out_shape=jax.ShapeDtypeStruct((rows, N), jnp.float32),
        in_specs=[anyspace, anyspace, vmem, vmem, vmem],
        out_specs=vmem,
        scratch_shapes=[
            pltpu.VMEM((R, K, V_row, N), jnp.bfloat16),
            pltpu.VMEM((C, K, V, N), jnp.bfloat16),
            pltpu.VMEM((2, K, V // 2, N), jnp.bfloat16),
            pltpu.VMEM((K, V, M), jnp.bfloat16),
            pltpu.VMEM((M, K * V), jnp.bfloat16),
            pltpu.VMEM((L, C, rows, N), jnp.float32),
            pltpu.VMEM((slots, C, rows, N), jnp.float32),
            pltpu.VMEM((C, rows, N), jnp.float32),
            dma((R, Q)), dma((R, Q)),
            dma((C, Q)), dma((C, Q)),
            dma((2, Q)), dma((2, Q)),
            dma((2, Q)), dma((2, Q)),
            dma((Q,)),
            dma((slots, C)), dma((slots, C)),
            dma((C,)), dma((C,)),
        ],
        compiler_params=pltpu.CompilerParams(collective_id=0, has_side_effects=True),
    )(integrals, amplitudes, coulomb, row_gap[:, None], col_gap[None, :])


def solution(mesh):
    R, C, L = (mesh.shape[a] for a in ("row", "col", "layer"))
    placed = (
        P("layer", "col", "row"),
        P("layer", "row", "col"),
        P(("row", "layer"), "col"),
        P(("row", "layer")),
        P("col"),
    )
    return jax.shard_map(
        functools.partial(local, R, C, L), mesh=mesh, in_specs=placed, out_specs=P(("row", "layer"), "col"),
        check_vma=False,
    )
```

time: 324 us -> 154 us (0.48)
  waiting for transfers between devices: 294 us -> 0 us
  Pallas kernels: 0 us -> 151 us
  between operations: 13.1 us -> 0.01 us
  matrix products: 9.85 us -> 0 us
    all_gather x2 -> x0, waiting for transfers between devices: 276 us -> none  [the longest x1 219 us: local(): lax.all_gather(integrals, 'col', axis=1, tiled=True)]
    pallas_call x0 -> x1, Pallas kernels: none -> 151 us  [local(): pl.pallas_call(functools.partial(kernel, R, C, L, Q), out_shape=jax.Shape...]
    reduce_scatter x1 -> x0, waiting for transfers between devices: 18.1 us -> none  [local(): lax.psum_scatter(partial_sum, 'layer', scatter_dimension=0, tiled=True)]
    dot_general x1 -> x0, matrix products: 9.85 us -> none  [local(): lax.dot_general(lax.all_gather(integrals, 'col', axis=1, tiled=True), gat...]
    unnamed x7 -> x1, local copies, waits for them, and re-layouts: 4.66 us -> 1.42 us
  transfers between devices with their start and end apart: 3 -> 0, of which waited for: 3 -> 0; matrix products, arithmetic and copies ran while one was open for 1% -> 0% of each run, Pallas kernels for 0% -> 0%
where the time goes in v1:
time: 154 us
  Pallas kernels  151 us (98%)
  local copies, waits for them, and re-layouts  2.79 us (2%)
    pallas_call x1, Pallas kernels, local(): pl.pallas_call(functools.partial(kernel, R, C, L, Q), out_shape=jax.Shape...  151 us

profile of v1, /device:TPU:0, one launch (start us, length us, event | category | flops | bytes accessed | tf_op | source)
XLA Modules:
  0.0 154.0 jit_solution(15099842285804011404)
XLA Ops:
  0.0 1.4 copy.6.rgap_ref
  1.4 151.2 %shard_map.55 = f32[96,128]{1,0:T(8,128)} custom-call(bf16[16,256,384]{2,1,0:T(8,128)(2,1)} %i_ref.1, bf16[16,512,128]{2,1,0:T(8,128)(2,1)} %a_ref.1, bf16[96,128]{1,0:T(8,128)(2,1)} %coul_ref.1, f32[96,1]{1,0:T(8,128)} %copy.6.rgap_ref, f32[1,128]{1,0:T(1,128)} %bitcast.3), custom_call_target="tpu_custom_call" | custom-call | tf_op jit(solution)/shard_map/pallas_call | solution.py:233
  152.6 1.4 copy.8

commit v2 on v0

v2 whole, which is shorter than its diff:
```python
import functools

import jax
import jax.numpy as jnp
from jax import lax
from jax.experimental import pallas as pl
from jax.experimental.pallas import tpu as pltpu
from jax.sharding import PartitionSpec as P

MESH = pl.DeviceIdType.MESH


def hi_order(n):
    if n == 1:
        return [0]
    below = hi_order(n // 2)
    return [2 * x + 1 for x in below] + [2 * x for x in below]


def kernel(R, C, L, Q, i_ref, a_ref, coul_ref, rgap_ref, cgap_ref, o_ref,
           a_all, az, i_all, i_t, acc, lay_buf, row_buf, col_buf,
           asend, arecv, xsend, xrecv, zsend, zrecv,
           osend, orecv, lsend, lrecv, rsend, rrecv, csend, crecv):
    r, c, l = lax.axis_index("row"), lax.axis_index("col"), lax.axis_index("layer")
    K, V_row, N = a_ref.shape
    V, M = i_ref.shape[1:]
    Kr = K // R
    kc = Kr // Q
    m = C // R
    w = kc * V
    rows = M // L
    stages = L.bit_length() - 1

    def remote(src, dst, ss, rs, **to):
        where = {"row": r, "col": c, "layer": l}
        where.update(to)
        return pltpu.make_async_remote_copy(src_ref=src, dst_ref=dst, send_sem=ss, recv_sem=rs,
                                            device_id=where, device_id_type=MESH)

    def ks(q):
        return pl.ds(q * kc, kc)

    def far_row(d):
        return lax.rem(r + d, R)

    def near(dc):
        return lax.rem(c + dc + C, C)

    order = sorted(range(1, C), key=lambda d: -min(d, C - d))

    def slice_for(d, q):
        return pl.ds(far_row(d) * Kr + q * kc, kc)

    def own_a(q):
        return pltpu.make_async_copy(a_ref.at[slice_for(0, q)], a_all.at[0, ks(q)], arecv.at[0, q])

    def own_i(q):
        return pltpu.make_async_copy(i_ref.at[slice_for(0, q)], i_all.at[0, ks(q)], xrecv.at[0, q])

    for q in range(Q):
        own_a(q).start()
        own_i(q).start()

    barrier = pltpu.get_barrier_semaphore()
    partners = [{"row": far_row(d)} for d in range(1, R)]
    partners += [{"col": near(d)} for d in range(1, C)]
    partners += [{"layer": l ^ (1 << t)} for t in range(stages)]
    for p in partners:
        where = {"row": r, "col": c, "layer": l}
        where.update(p)
        pl.semaphore_signal(barrier, inc=1, device_id=where, device_id_type=MESH)
    pl.semaphore_wait(barrier, len(partners))

    def row_a(d, q):
        return remote(a_ref.at[slice_for(d, q)], a_all.at[R - d, ks(q)], asend.at[d, q], arecv.at[R - d, q], row=far_row(d))

    def row_i(d, q):
        return remote(i_ref.at[slice_for(d, q)], i_all.at[R - d, ks(q)], xsend.at[d, q], xrecv.at[R - d, q], row=far_row(d))

    def col_a(d, j, q):
        b = far_row(d) * m + j
        at = pl.ds(j * V, V)
        src = a_all.at[d, ks(q), at] if d else a_ref.at[slice_for(0, q), at]
        return b, remote(src, az.at[c, ks(q)], zsend.at[d, j, q], zrecv.at[c, q], col=b)

    def col_start(d, q):
        for j in range(m):
            b, cp = col_a(d, j, q)

            @pl.when(b != c)
            def _():
                cp.start()

    for q in range(Q):
        for d in range(1, R):
            row_a(d, q).start()
        col_start(0, q)
    for q in range(Q):
        for d in range(1, R):
            row_i(d, q).start()

    def turn(d, q):
        for k in range(kc):
            at = (q * kc + k) * V
            i_t[d, :, at:at + V] = i_all[d, q * kc + k].T

    def add(d, block, x, q):
        part = lax.dot_general(i_t[d, :, q * w:(q + 1) * w], x, (((1,), (0,)), ((), ())),
                               preferred_element_type=jnp.float32)
        for lb in range(L):
            piece = part[lb * rows:(lb + 1) * rows]
            if q == 0:
                acc[d, lb, block] = piece
            else:
                acc[d, lb, block] += piece

    own_row = lax.rem(lax.div(c, m) - r + R, R)
    own_at = pl.ds(pl.multiple_of(lax.rem(c, m) * V, V), V)

    def own_block(d, q):
        add(d, c, a_all[own_row, ks(q), own_at].reshape(w, N), q)

    for q in range(Q):
        own_a(q).wait()
        for d in range(1, R):
            row_a(R - d, q).wait_recv()
            col_start(d, q)
        own_i(q).wait()
        turn(0, q)
        own_block(0, q)

    for q in range(Q):
        for dc in order[::-1]:
            s = near(dc)
            here = az.at[s, ks(q)]
            remote(here, here, zsend.at[0, 0, q], zrecv.at[s, q], col=s).wait_recv()
            add(0, s, az[s, ks(q)].reshape(w, N), q)

    def block(t, hi, bit):
        return (hi << (t + 1)) | (bit << t) | (l & ((1 << t) - 1))

    def halving(d, t, i, col):
        n = L >> (t + 1)
        hi = (l >> (t + 1)) ^ hi_order(n)[i]
        bit = (l >> t) & 1
        slot = n - 1 + hi
        give, keep = block(t, hi, 1 - bit), block(t, hi, bit)
        if d == 0:
            cp = remote(acc.at[0, give], lay_buf.at[0, slot], osend.at[slot], orecv.at[slot], layer=l ^ (1 << t))
        else:
            cp = remote(acc.at[d, give, col], lay_buf.at[d, slot, col], lsend.at[d, slot, col], lrecv.at[d, slot, col],
                        layer=l ^ (1 << t))
        return cp, keep, slot

    def own_stage(t):
        for i in range(L >> (t + 1)):
            cp, keep, slot = halving(0, t, i, None)
            cp.wait_recv()
            acc[0, keep] += lay_buf[0, slot]
            if t + 1 < stages and i < L >> (t + 2):
                halving(0, t + 1, i, None)[0].start()

    for i in range(L >> 1):
        halving(0, 0, i, None)[0].start()

    for q in range(Q):
        for d in range(1, R):
            row_i(R - d, q).wait_recv()
            turn(d, q)
            own_block(d, q)
            for dc in order:
                s = near(dc)
                add(d, s, az[s, ks(q)].reshape(w, N), q)
        if q == 0:
            own_stage(0)

    c_order = [near(dc) for dc in order] + [c]

    def row_sum(d, col):
        return remote(acc.at[d, l, col], row_buf.at[R - d, col], rsend.at[d, col], rrecv.at[R - d, col], row=far_row(d))

    def col_sum(dc):
        return remote(acc.at[0, l, near(dc)], col_buf.at[c], csend.at[dc], crecv.at[c], col=near(dc))

    for i in range(L >> 1):
        for d in range(1, R):
            for col in c_order:
                halving(d, 0, i, col)[0].start()
    for t in range(1, stages):
        own_stage(t)
    for t in range(stages):
        for i in range(L >> (t + 1)):
            for d in range(1, R):
                for col in c_order:
                    cp, keep, slot = halving(d, t, i, col)
                    cp.wait_recv()
                    acc[d, keep, col] += lay_buf[d, slot, col]
                    if t + 1 == stages:
                        row_sum(d, col).start()
                    elif i < L >> (t + 2):
                        halving(d, t + 1, i, col)[0].start()
    for at, col in enumerate(c_order):
        for d in range(1, R):
            row_sum(R - d, col).wait_recv()
            acc[0, l, col] += row_buf[d, col]
        if at < C - 1:
            col_sum(order[at]).start()

    total = acc[0, l, c]
    for dc in order[::-1]:
        s = near(dc)
        remote(col_buf.at[s], col_buf.at[s], csend.at[dc], crecv.at[s], col=s).wait_recv()
        total += col_buf[s]
    o_ref[...] = (coul_ref[...].astype(jnp.float32) + total) / (rgap_ref[...] + cgap_ref[...])

    for q in range(Q):
        for d in range(R):
            if d:
                row_a(d, q).wait_send()
                row_i(d, q).wait_send()
            for j in range(m):
                b, cp = col_a(d, j, q)

                @pl.when(b != c)
                def _():
                    cp.wait_send()
    for t in range(stages):
        for i in range(L >> (t + 1)):
            halving(0, t, i, None)[0].wait_send()
            for d in range(1, R):
                for col in c_order:
                    halving(d, t, i, col)[0].wait_send()
    for col in c_order:
        for d in range(1, R):
            row_sum(d, col).wait_send()
    for dc in order:
        col_sum(dc).wait_send()


def local(R, C, L, integrals, amplitudes, coulomb, row_gap, col_gap):
    K, V, M = integrals.shape
    V_row, N = amplitudes.shape[1:]
    rows = M // L
    Kr = K // R
    Q = Kr
    m = C // R
    slots = L - 1
    dma = pltpu.SemaphoreType.DMA
    vmem = pl.BlockSpec(memory_space=pltpu.VMEM)
    anyspace = pl.BlockSpec(memory_space=pl.ANY)
    return pl.pallas_call(
        functools.partial(kernel, R, C, L, Q),
        out_shape=jax.ShapeDtypeStruct((rows, N), jnp.float32),
        in_specs=[anyspace, anyspace, vmem, vmem, vmem],
        out_specs=vmem,
        scratch_shapes=[
            pltpu.VMEM((R, Kr, V_row, N), jnp.bfloat16),
            pltpu.VMEM((C, Kr, V, N), jnp.bfloat16),
            pltpu.VMEM((R, Kr, V, M), jnp.bfloat16),
            pltpu.VMEM((R, M, Kr * V), jnp.bfloat16),
            pltpu.VMEM((R, L, C, rows, N), jnp.float32),
            pltpu.VMEM((R, slots, C, rows, N), jnp.float32),
            pltpu.VMEM((R, C, rows, N), jnp.float32),
            pltpu.VMEM((C, rows, N), jnp.float32),
            dma((R, Q)), dma((R, Q)),
            dma((R, Q)), dma((R, Q)),
            dma((R, m, Q)), dma((C, Q)),
            dma((slots,)), dma((slots,)),
            dma((R, slots, C)), dma((R, slots, C)),
            dma((R, C)), dma((R, C)),
            dma((C,)), dma((C,)),
        ],
        compiler_params=pltpu.CompilerParams(collective_id=0, has_side_effects=True),
    )(integrals, amplitudes, coulomb, row_gap[:, None], col_gap[None, :])


def solution(mesh):
    R, C, L = (mesh.shape[a] for a in ("row", "col", "layer"))
    placed = (
        P("layer", "col", "row"),
        P("layer", "row", "col"),
        P(("row", "layer"), "col"),
        P(("row", "layer")),
        P("col"),
    )
    return jax.shard_map(
        functools.partial(local, R, C, L), mesh=mesh, in_specs=placed, out_specs=P(("row", "layer"), "col"),
        check_vma=False,
    )
```

time: 324 us -> 83.1 us (0.26)
  waiting for transfers between devices: 294 us -> 0 us
  Pallas kernels: 0 us -> 80 us
  between operations: 13.1 us -> 0.01 us
  matrix products: 9.85 us -> 0 us
    all_gather x2 -> x0, waiting for transfers between devices: 276 us -> none  [the longest x1 219 us: local(): lax.all_gather(integrals, 'col', axis=1, tiled=True)]
    pallas_call x0 -> x1, Pallas kernels: none -> 80 us  [local(): pl.pallas_call(functools.partial(kernel, R, C, L, Q), out_shape=jax.Shape...]
    reduce_scatter x1 -> x0, waiting for transfers between devices: 18.1 us -> none  [local(): lax.psum_scatter(partial_sum, 'layer', scatter_dimension=0, tiled=True)]
    dot_general x1 -> x0, matrix products: 9.85 us -> none  [local(): lax.dot_general(lax.all_gather(integrals, 'col', axis=1, tiled=True), gat...]
    unnamed x7 -> x1, local copies, waits for them, and re-layouts: 4.66 us -> 1.42 us
  transfers between devices with their start and end apart: 3 -> 0, of which waited for: 3 -> 0; matrix products, arithmetic and copies ran while one was open for 1% -> 0% of each run, Pallas kernels for 0% -> 0%
where the time goes in v2:
time: 83.1 us; the launch traced here: 82.8 us
  Pallas kernels  80 us (96%)
  local copies, waits for them, and re-layouts  2.79 us (3%)
    pallas_call x1, Pallas kernels, local(): pl.pallas_call(functools.partial(kernel, R, C, L, Q), out_shape=jax.Shape...  80 us

profile of v2, /device:TPU:0, one launch (start us, length us, event | category | flops | bytes accessed | tf_op | source)
XLA Modules:
  0.0 82.8 jit_solution(2591020744008466616)
XLA Ops:
  0.0 1.4 %copy.6.rgap_ref = f32[96,1]{1,0:T(8,128)} copy(f32[96,1]{0,1:T(1,128)} %bitcast.2) | data formatting | bytes 768 | tf_op jit(solution)/shard_map/broadcast_in_dim | solution.py:274
  1.4 80.0 %shard_map.55 = f32[96,128]{1,0:T(8,128)} custom-call(bf16[16,256,384]{2,1,0:T(8,128)(2,1)} %i_ref.1, bf16[16,512,128]{2,1,0:T(8,128)(2,1)} %a_ref.1, bf16[96,128]{1,0:T(8,128)(2,1)} %coul_ref.1, f32[96,1]{1,0:T(8,128)} %copy.6.rgap_ref, f32[1,128]{1,0:T(1,128)} %bitcast.3), custom_call_target="tpu_custom_call" | custom-call | tf_op jit(solution)/shard_map/pallas_call | solution.py:251
  81.4 1.4 %copy.8 = f32[96,128]{1,0:T(8,128)} copy(f32[96,128]{1,0:T(8,128)} %shard_map.55) | data formatting | bytes 98304

commit v3 on v2

--- a/solution.py
+++ b/solution.py
@@ -17,7 +17,7 @@
     return [2 * x + 1 for x in below] + [2 * x for x in below]
 
 
-def kernel(R, C, L, Q, i_ref, a_ref, coul_ref, rgap_ref, cgap_ref, o_ref,
+def kernel(R, C, L, Q, i_ref, a_ref, o_ref,
            a_all, az, i_all, i_t, acc, lay_buf, row_buf, col_buf,
            asend, arecv, xsend, xrecv, zsend, zrecv,
            osend, orecv, lsend, lrecv, rsend, rrecv, csend, crecv):
@@ -30,6 +30,9 @@
     w = kc * V
     rows = M // L
     stages = L.bit_length() - 1
+    late = M // 2 // 128 * 128 if stages == 2 and M % 128 == 0 else 0
+    early = M - late
+    top = l >> (stages - 1)
 
     def remote(src, dst, ss, rs, **to):
         where = {"row": r, "col": c, "layer": l}
@@ -74,8 +77,13 @@
     def row_a(d, q):
         return remote(a_ref.at[slice_for(d, q)], a_all.at[R - d, ks(q)], asend.at[d, q], arecv.at[R - d, q], row=far_row(d))
 
-    def row_i(d, q):
-        return remote(i_ref.at[slice_for(d, q)], i_all.at[R - d, ks(q)], xsend.at[d, q], xrecv.at[R - d, q], row=far_row(d))
+    parts = [(0, early, (1 - top) * late)] + ([(early, late, top * early)] if late else [])
+
+    def row_i(d, q, p):
+        at, size, start = parts[p]
+        src = i_ref.at[slice_for(d, q), :, pl.ds(pl.multiple_of(start, 128), size)] if late else i_ref.at[slice_for(d, q)]
+        return remote(src, i_all.at[R - d, ks(q), :, pl.ds(at, size)], xsend.at[p * R + d, q], xrecv.at[p * R + R - d, q],
+                      row=far_row(d))
 
     def col_a(d, j, q):
         b = far_row(d) * m + j
@@ -95,30 +103,34 @@
         for d in range(1, R):
             row_a(d, q).start()
         col_start(0, q)
-    for q in range(Q):
-        for d in range(1, R):
-            row_i(d, q).start()
-
-    def turn(d, q):
+    for p in range(len(parts)):
+        for q in range(Q):
+            for d in range(1, R):
+                row_i(d, q, p).start()
+
+    whole = (0, M, 0)
+
+    def turn(d, q, part):
+        first, size = part[:2]
         for k in range(kc):
             at = (q * kc + k) * V
-            i_t[d, :, at:at + V] = i_all[d, q * kc + k].T
-
-    def add(d, block, x, q):
-        part = lax.dot_general(i_t[d, :, q * w:(q + 1) * w], x, (((1,), (0,)), ((), ())),
-                               preferred_element_type=jnp.float32)
-        for lb in range(L):
-            piece = part[lb * rows:(lb + 1) * rows]
-            if q == 0:
-                acc[d, lb, block] = piece
-            else:
-                acc[d, lb, block] += piece
+            i_t[d, first:first + size, at:at + V] = i_all[d, q * kc + k, :, first:first + size].T
+
+    def add(d, block, x, q, part):
+        first, size, start = part
+        piece = lax.dot_general(i_t[d, first:first + size, q * w:(q + 1) * w], x, (((1,), (0,)), ((), ())),
+                                preferred_element_type=jnp.float32)
+        to = pl.ds(start if isinstance(start, int) else pl.multiple_of(start, 128), size)
+        if q == 0:
+            acc[d, block, to] = piece
+        else:
+            acc[d, block, to] += piece
 
     own_row = lax.rem(lax.div(c, m) - r + R, R)
     own_at = pl.ds(pl.multiple_of(lax.rem(c, m) * V, V), V)
 
-    def own_block(d, q):
-        add(d, c, a_all[own_row, ks(q), own_at].reshape(w, N), q)
+    def own_block(d, q, part):
+        add(d, c, a_all[own_row, ks(q), own_at].reshape(w, N), q, part)
 
     for q in range(Q):
         own_a(q).wait()
@@ -126,15 +138,15 @@
             row_a(R - d, q).wait_recv()
             col_start(d, q)
         own_i(q).wait()
-        turn(0, q)
-        own_block(0, q)
+        turn(0, q, whole)
+        own_block(0, q, whole)
 
     for q in range(Q):
         for dc in order[::-1]:
             s = near(dc)
             here = az.at[s, ks(q)]
             remote(here, here, zsend.at[0, 0, q], zrecv.at[s, q], col=s).wait_recv()
-            add(0, s, az[s, ks(q)].reshape(w, N), q)
+            add(0, s, az[s, ks(q)].reshape(w, N), q, whole)
 
     def block(t, hi, bit):
         return (hi << (t + 1)) | (bit << t) | (l & ((1 << t) - 1))
@@ -145,10 +157,11 @@
         bit = (l >> t) & 1
         slot = n - 1 + hi
         give, keep = block(t, hi, 1 - bit), block(t, hi, bit)
+        give, keep = (pl.ds(pl.multiple_of(b * rows, 8), rows) for b in (give, keep))
         if d == 0:
-            cp = remote(acc.at[0, give], lay_buf.at[0, slot], osend.at[slot], orecv.at[slot], layer=l ^ (1 << t))
+            cp = remote(acc.at[0, :, give], lay_buf.at[0, slot], osend.at[slot], orecv.at[slot], layer=l ^ (1 << t))
         else:
-            cp = remote(acc.at[d, give, col], lay_buf.at[d, slot, col], lsend.at[d, slot, col], lrecv.at[d, slot, col],
+            cp = remote(acc.at[d, col, give], lay_buf.at[d, slot, col], lsend.at[d, slot, col], lrecv.at[d, slot, col],
                         layer=l ^ (1 << t))
         return cp, keep, slot
 
@@ -156,68 +169,83 @@
         for i in range(L >> (t + 1)):
             cp, keep, slot = halving(0, t, i, None)
             cp.wait_recv()
-            acc[0, keep] += lay_buf[0, slot]
+            acc[0, :, keep] += lay_buf[0, slot]
             if t + 1 < stages and i < L >> (t + 2):
                 halving(0, t + 1, i, None)[0].start()
 
     for i in range(L >> 1):
         halving(0, 0, i, None)[0].start()
 
-    for q in range(Q):
-        for d in range(1, R):
-            row_i(R - d, q).wait_recv()
-            turn(d, q)
-            own_block(d, q)
-            for dc in order:
-                s = near(dc)
-                add(d, s, az[s, ks(q)].reshape(w, N), q)
-        if q == 0:
-            own_stage(0)
-
     c_order = [near(dc) for dc in order] + [c]
-
-    def row_sum(d, col):
-        return remote(acc.at[d, l, col], row_buf.at[R - d, col], rsend.at[d, col], rrecv.at[R - d, col], row=far_row(d))
-
-    def col_sum(dc):
-        return remote(acc.at[0, l, near(dc)], col_buf.at[c], csend.at[dc], crecv.at[c], col=near(dc))
-
-    for i in range(L >> 1):
+    mine = pl.ds(pl.multiple_of(l * rows, 8), rows)
+
+    def first_stage_start(i):
         for d in range(1, R):
             for col in c_order:
                 halving(d, 0, i, col)[0].start()
+
+    def stage_end(t, i):
+        for d in range(1, R):
+            for col in c_order:
+                cp, keep, slot = halving(d, t, i, col)
+                cp.wait_recv()
+                acc[d, col, keep] += lay_buf[d, slot, col]
+                if t + 1 == stages:
+                    row_sum(d, col).start()
+                elif i < L >> (t + 2):
+                    halving(d, t + 1, i, col)[0].start()
+
+    for p, part in enumerate(parts):
+        for q in range(Q):
+            for d in range(1, R):
+                row_i(R - d, q, p).wait_recv()
+                turn(d, q, part)
+                own_block(d, q, part)
+                for dc in order:
+                    s = near(dc)
+                    add(d, s, az[s, ks(q)].reshape(w, N), q, part)
+            if p == 0 and q == 0:
+                own_stage(0)
+            if p == 1 and q == min(1, Q - 1):
+                stage_end(0, 0)
+        if late:
+            first_stage_start(p)
+
+    def row_sum(d, col):
+        return remote(acc.at[d, col, mine], row_buf.at[R - d, col], rsend.at[d, col], rrecv.at[R - d, col], row=far_row(d))
+
+    def col_sum(dc):
+        return remote(acc.at[0, near(dc), mine], col_buf.at[c], csend.at[dc], crecv.at[c], col=near(dc))
+
+    if not late:
+        for i in range(L >> 1):
+            first_stage_start(i)
     for t in range(1, stages):
         own_stage(t)
     for t in range(stages):
         for i in range(L >> (t + 1)):
-            for d in range(1, R):
-                for col in c_order:
-                    cp, keep, slot = halving(d, t, i, col)
-                    cp.wait_recv()
-                    acc[d, keep, col] += lay_buf[d, slot, col]
-                    if t + 1 == stages:
-                        row_sum(d, col).start()
-                    elif i < L >> (t + 2):
-                        halving(d, t + 1, i, col)[0].start()
+            if not (late and t == 0 and i == 0):
+                stage_end(t, i)
     for at, col in enumerate(c_order):
         for d in range(1, R):
             row_sum(R - d, col).wait_recv()
-            acc[0, l, col] += row_buf[d, col]
+            acc[0, col, mine] += row_buf[d, col]
         if at < C - 1:
             col_sum(order[at]).start()
 
-    total = acc[0, l, c]
+    total = acc[0, c, mine]
     for dc in order[::-1]:
         s = near(dc)
         remote(col_buf.at[s], col_buf.at[s], csend.at[dc], crecv.at[s], col=s).wait_recv()
         total += col_buf[s]
-    o_ref[...] = (coul_ref[...].astype(jnp.float32) + total) / (rgap_ref[...] + cgap_ref[...])
+    o_ref[...] = total
 
     for q in range(Q):
         for d in range(R):
             if d:
                 row_a(d, q).wait_send()
-                row_i(d, q).wait_send()
+                for p in range(len(parts)):
+                    row_i(d, q, p).wait_send()
             for j in range(m):
                 b, cp = col_a(d, j, q)
 
@@ -248,22 +276,22 @@
     dma = pltpu.SemaphoreType.DMA
     vmem = pl.BlockSpec(memory_space=pltpu.VMEM)
     anyspace = pl.BlockSpec(memory_space=pl.ANY)
-    return pl.pallas_call(
+    own_rows = pl.pallas_call(
         functools.partial(kernel, R, C, L, Q),
         out_shape=jax.ShapeDtypeStruct((rows, N), jnp.float32),
-        in_specs=[anyspace, anyspace, vmem, vmem, vmem],
+        in_specs=[anyspace, anyspace],
         out_specs=vmem,
         scratch_shapes=[
             pltpu.VMEM((R, Kr, V_row, N), jnp.bfloat16),
             pltpu.VMEM((C, Kr, V, N), jnp.bfloat16),
             pltpu.VMEM((R, Kr, V, M), jnp.bfloat16),
             pltpu.VMEM((R, M, Kr * V), jnp.bfloat16),
-            pltpu.VMEM((R, L, C, rows, N), jnp.float32),
+            pltpu.VMEM((R, C, M, N), jnp.float32),
             pltpu.VMEM((R, slots, C, rows, N), jnp.float32),
             pltpu.VMEM((R, C, rows, N), jnp.float32),
             pltpu.VMEM((C, rows, N), jnp.float32),
             dma((R, Q)), dma((R, Q)),
-            dma((R, Q)), dma((R, Q)),
+            dma((2 * R, Q)), dma((2 * R, Q)),
             dma((R, m, Q)), dma((C, Q)),
             dma((slots,)), dma((slots,)),
             dma((R, slots, C)), dma((R, slots, C)),
@@ -271,7 +299,9 @@
             dma((C,)), dma((C,)),
         ],
         compiler_params=pltpu.CompilerParams(collective_id=0, has_side_effects=True),
-    )(integrals, amplitudes, coulomb, row_gap[:, None], col_gap[None, :])
+    )(integrals, amplitudes)
+    gap_sum = row_gap[:, None] + col_gap[None, :]
+    return (coulomb.astype(jnp.float32) + own_rows) / gap_sum
 
 
 def solution(mesh):

time: 83.1 us -> 79.5 us (0.957)
  local copies, waits for them, and re-layouts: 2.79 us -> 0.01 us
  Pallas kernels: 80 us -> 77.8 us
  other arithmetic: 0 us -> 1.51 us
    pallas_call x1, Pallas kernels: 80 us -> 77.8 us  [local(): pl.pallas_call(functools.partial(kernel, R, C, L, Q), out_shape=jax.Shape...]
    div x0 -> x1, other arithmetic: none -> 1.51 us  [local(): return (coulomb.astype(jnp.float32) + own_rows) / gap_sum]
    unnamed x1 -> x6, local copies, waits for them, and re-layouts: 1.42 us -> 0.01 us
    broadcast_in_dim x1 -> x0, local copies, waits for them, and re-layouts: 1.37 us -> none  [local(): row_gap[:, None]]
where the time goes in v3:
time: 79.5 us; the launch traced here: 79.3 us
  Pallas kernels  77.8 us (98%)
  other arithmetic  1.51 us (2%)
    pallas_call x1, Pallas kernels, local(): pl.pallas_call(functools.partial(kernel, R, C, L, Q), out_shape=jax.Shape...  77.8 us

profile of v3, /device:TPU:0, one launch (start us, length us, event | category | flops | bytes accessed | tf_op | source)
XLA Modules:
  0.0 79.3 jit_solution(8728039810485779628)
XLA Ops:
  0.0 0.0 copy-start.1
  0.0 0.0 copy-start.2
  0.0 0.0 copy-start
  0.0 77.8 %shard_map.55 = f32[96,128]{1,0:T(8,128)} custom-call(bf16[16,256,384]{2,1,0:T(8,128)(2,1)} %i_ref.1, bf16[16,512,128]{2,1,0:T(8,128)(2,1)} %a_ref.1), custom_call_target="tpu_custom_call" | custom-call | tf_op jit(solution)/shard_map/pallas_call | solution.py:279
  77.8 0.0 copy-done.1
  77.8 0.0 copy-done.2
  77.8 0.0 copy-done
  77.8 1.5 %add_divide_fusion = f32[96,128]{1,0:T(8,128)} fusion(f32[96,128]{1,0:T(8,128)} %shard_map.55, bf16[96,128]{1,0:T(8,128)(2,1)S(1)} %copy-done, f32[128]{0:T(128)S(1)} %copy-done.1, f32[96]{0:T(128)S(1)} %copy-done.2), kind=kLoop, calls=%fused_computation | loop fusion | flops 49152 | bytes 123776 | tf_op jit(solution)/shard_map/div | solution.py:304
Async XLA Ops:
  0.0 77.8 %copy-start.1 = (f32[128]{0:T(128)S(1)}, f32[128]{0:T(128)}, u32[]{:S(2)}) copy-start(f32[128]{0:T(128)} %param.9) | copy-start | bytes 1540
  0.0 77.8 %copy-start.2 = (f32[96]{0:T(128)S(1)}, f32[96]{0:T(128)}, u32[]{:S(2)}) copy-start(f32[96]{0:T(128)} %param.8) | copy-start | bytes 1156
  0.0 77.8 %copy-start = (bf16[96,128]{1,0:T(8,128)(2,1)S(1)}, bf16[96,128]{1,0:T(8,128)(2,1)}, u32[]{:S(2)}) copy-start(bf16[96,128]{1,0:T(8,128)(2,1)} %param.7) | copy-start | bytes 73732

commit v4 on v3

--- a/solution.py
+++ b/solution.py
@@ -65,8 +65,7 @@
         own_i(q).start()
 
     barrier = pltpu.get_barrier_semaphore()
-    partners = [{"row": far_row(d)} for d in range(1, R)]
-    partners += [{"col": near(d)} for d in range(1, C)]
+    partners = [{"row": far_row(d), "col": near(dc)} for d in range(R) for dc in range(C) if d or dc]
     partners += [{"layer": l ^ (1 << t)} for t in range(stages)]
     for p in partners:
         where = {"row": r, "col": c, "layer": l}
@@ -212,7 +211,8 @@
             first_stage_start(p)
 
     def row_sum(d, col):
-        return remote(acc.at[d, col, mine], row_buf.at[R - d, col], rsend.at[d, col], rrecv.at[R - d, col], row=far_row(d))
+        return remote(acc.at[d, col, mine], row_buf.at[R - d, c], rsend.at[d, col], rrecv.at[R - d, c],
+                      row=far_row(d), col=col)
 
     def col_sum(dc):
         return remote(acc.at[0, near(dc), mine], col_buf.at[c], csend.at[dc], crecv.at[c], col=near(dc))
@@ -222,22 +222,22 @@
             first_stage_start(i)
     for t in range(1, stages):
         own_stage(t)
+    for dc in order:
+        col_sum(dc).start()
     for t in range(stages):
         for i in range(L >> (t + 1)):
             if not (late and t == 0 and i == 0):
                 stage_end(t, i)
-    for at, col in enumerate(c_order):
-        for d in range(1, R):
-            row_sum(R - d, col).wait_recv()
-            acc[0, col, mine] += row_buf[d, col]
-        if at < C - 1:
-            col_sum(order[at]).start()
-
     total = acc[0, c, mine]
     for dc in order[::-1]:
         s = near(dc)
         remote(col_buf.at[s], col_buf.at[s], csend.at[dc], crecv.at[s], col=s).wait_recv()
         total += col_buf[s]
+    for col in c_order[::-1]:
+        for d in range(1, R):
+            here = row_buf.at[d, col]
+            remote(here, here, rsend.at[d, col], rrecv.at[d, col], row=far_row(d), col=col).wait_recv()
+            total += row_buf[d, col]
     o_ref[...] = total
 
     for q in range(Q):

time: 79.5 us -> 78.6 us (0.989)
  Pallas kernels: 77.8 us -> 76.9 us
    pallas_call x1, Pallas kernels: 77.8 us -> 76.9 us  [local(): pl.pallas_call(functools.partial(kernel, R, C, L, Q), out_shape=jax.Shape...]
where the time goes in v4:
time: 78.6 us; the launch traced here: 78.4 us
  Pallas kernels  76.9 us (98%)
  other arithmetic  1.51 us (2%)
    pallas_call x1, Pallas kernels, local(): pl.pallas_call(functools.partial(kernel, R, C, L, Q), out_shape=jax.Shape...  76.9 us

profile of v4, /device:TPU:0, one launch (start us, length us, event | category | flops | bytes accessed | tf_op | source)
XLA Modules:
  0.0 78.4 jit_solution(14986146369940208762)
XLA Ops:
  0.0 0.0 copy-start.1
  0.0 0.0 copy-start.2
  0.0 0.0 copy-start
  0.0 76.9 %shard_map.55 = f32[96,128]{1,0:T(8,128)} custom-call(bf16[16,256,384]{2,1,0:T(8,128)(2,1)} %i_ref.1, bf16[16,512,128]{2,1,0:T(8,128)(2,1)} %a_ref.1), custom_call_target="tpu_custom_call" | custom-call | tf_op jit(solution)/shard_map/pallas_call | solution.py:279
  76.9 0.0 copy-done.1
  76.9 0.0 copy-done.2
  76.9 0.0 copy-done
  76.9 1.5 %add_divide_fusion = f32[96,128]{1,0:T(8,128)} fusion(f32[96,128]{1,0:T(8,128)} %shard_map.55, bf16[96,128]{1,0:T(8,128)(2,1)S(1)} %copy-done, f32[128]{0:T(128)S(1)} %copy-done.1, f32[96]{0:T(128)S(1)} %copy-done.2), kind=kLoop, calls=%fused_computation | loop fusion | flops 49152 | bytes 123776 | tf_op jit(solution)/shard_map/div | solution.py:304
Async XLA Ops:
  0.0 76.9 %copy-start.1 = (f32[128]{0:T(128)S(1)}, f32[128]{0:T(128)}, u32[]{:S(2)}) copy-start(f32[128]{0:T(128)} %param.9) | copy-start | bytes 1540
  0.0 76.9 %copy-start.2 = (f32[96]{0:T(128)S(1)}, f32[96]{0:T(128)}, u32[]{:S(2)}) copy-start(f32[96]{0:T(128)} %param.8) | copy-start | bytes 1156
  0.0 76.9 %copy-start = (bf16[96,128]{1,0:T(8,128)(2,1)S(1)}, bf16[96,128]{1,0:T(8,128)(2,1)}, u32[]{:S(2)}) copy-start(bf16[96,128]{1,0:T(8,128)(2,1)} %param.7) | copy-start | bytes 73732
